TPU v7x, 32 devices: a whole 2x2x4 slice. The times are simulated.
32 devices in a mesh: sub: 8 (over z, x), col: 4 (over y, core).
Axes of the slice: x: 2, y: 2, z: 4, core: 2. Of those that a mesh axis runs over, the one named last changes fastest.
Arguments:
- adjoint_source: float32 [64, 12288], P('col', 'sub'), may hold values from -4 to 4
- start_field: float32 [64, 12288], P('col', 'sub'), may hold values from -3 to 3
- row_diagonal: float32 [12288], P('sub'), may hold values from 2 to 4
- row_values: float32 [26, 12288], P(None, 'sub'), may hold values from -0.6 to 0.6
- row_columns: int32 [26, 12288], P(None, 'sub'), may hold values from 0 to 2047
- weight_code: int32 [16384], P('sub'), may hold values from 0 to 3
- slot_count: int32 [8, 4], P('sub'), may hold values from 0 to 128, as said below
- slot_rows: int32 [8, 4, 128], P('sub'), may hold values from 0 to 1535, as said below
- local_inverse: float32 [16384, 2048], P(('sub', 'col')), may hold values from -0.006629126 to 0.60662913
- coarse_modes: float32 [4, 12288], P(None, 'sub'), may hold values from -0.15309311 to 0.15309311
- coarse_inverse: float32 [32, 32], P('sub'), may hold values from -0.079549513 to 0.6795495
Outputs:
- adjoint: float32 [64, 12288], P('col', 'sub')
Inputs may be any that keep to these rules, and one draw needn't show every extreme that they name: slot_count[s, d] counts the live slots that subdomain s takes from subdomain s - 2, s - 1, s + 1, s + 2 for d = 0, 1, 2, 3; it is zero where that subdomain does not exist, and some entry equals 128 in every draw. `slot_rows`: the entries of one subdomain and direction are distinct.
All inputs are finite; a program needn't handle non-finite values.
Results may differ from a plain program's by a relative error of at most 0.00016.
Values sent between devices are 32-bit elements; how exact they have to be, the bound alone decides.
A program may use at most 128 MiB of HBM per device.

v0:
```python
import functools

import jax
import jax.numpy as jnp
from jax import lax
from jax.experimental import pallas as pl
from jax.experimental.pallas import tpu as pltpu
from jax.sharding import PartitionSpec as P

ITERS = 3
LANES = 128
SUBLANES = 8

direction_steps = (-2, -1, 1, 2)
damping = 0.7
highest = lax.Precision.HIGHEST
contract_last = (((1,), (1,)), ((), ()))
f32 = jnp.float32
bf16 = jnp.bfloat16
DIRS = len(direction_steps)
GROUPS = 2


def lane_gather(tile, low):
    return jnp.take_along_axis(tile, low, axis=1, mode="promise_in_bounds")


def split(x):
    high = x.astype(bf16)
    return high, (x - high.astype(f32)).astype(bf16)


def kernel(
    subs, cols,
    source_ref, start_ref, diag_ref, vals_ref, idx_ref, code_ref, count_ref, rows_ref, modes_ref, cinv_ref, li_hbm,
    out_ref,
    lam, idx_tiles, val_tiles, li, li_hi, li_lo, table, tables, fidx, inverse, cinv_pad, cinv_turned,
    halo_out, halo_in, own_x, mar_out, mar_x, coarse_x, solved, sol_in, ret_in,
    li_sem, tab_s, tab_r, halo_s, halo_r, own_s, own_r, mar_s, mar_r, co_s, co_r, sol_s, sol_r, ret_s, ret_r,
):
    s = lax.axis_index("sub")
    c = lax.axis_index("col")
    owned = start_ref.shape[1]
    rows = lam.shape[1]
    tiles = owned // LANES
    early = tiles // 2
    terms = vals_ref.shape[0]
    block = li_hbm.shape[0]
    nmodes = modes_ref.shape[0]
    cuts = ((0, early * LANES), (early * LANES, owned - early * LANES))

    def sub_at(by):
        return lax.rem(s + (by + subs), subs)

    def col_at(by):
        return lax.rem(c + (by + cols), cols)

    def inside(by):
        return jnp.logical_and(s + by >= 0, s + by < subs)

    def remote(src, dst, send, recv, where):
        return pltpu.make_async_remote_copy(
            src_ref=src, dst_ref=dst, send_sem=send, recv_sem=recv,
            device_id=where, device_id_type=pl.DeviceIdType.MESH,
        )

    load_inverse = pltpu.make_async_copy(li_hbm, li, li_sem)
    load_inverse.start()

    partners = []
    for step in range(1, cols):
        partners.append((0, step))
    for by in range(1, subs):
        near = by in (1, 2, subs - 1, subs - 2)
        for step in range(cols if near else 1):
            partners.append((by, step))
    barrier = pltpu.get_barrier_semaphore()
    tables[...] = jnp.full(tables.shape, -1, jnp.int32)
    for clean in (halo_in, mar_x, ret_in, coarse_x):
        clean[...] = jnp.zeros_like(clean)
    for by, step in partners:
        pl.semaphore_signal(
            barrier, inc=1, device_id=(sub_at(by), col_at(step)), device_id_type=pl.DeviceIdType.MESH
        )
    lane = lax.broadcasted_iota(jnp.int32, (1, LANES), 1)
    for d in range(DIRS):
        table[pl.ds(d, 1), :] = jnp.where(lane < count_ref[0, d], rows_ref[0, pl.ds(d, 1), :], -1)
    for g in range(GROUPS):
        lam[g] = start_ref[g * rows : (g + 1) * rows, :]
    for t in range(tiles):
        idx_tiles[t] = idx_ref[:, t * LANES : (t + 1) * LANES]
        val_tiles[t] = vals_ref[:, t * LANES : (t + 1) * LANES]
    members = subs * nmodes
    cinv_pad[...] = jnp.zeros_like(cinv_pad)
    cinv_pad[pl.ds(0, nmodes), :] = cinv_ref[...]
    square = (members, members)
    same = lax.broadcasted_iota(jnp.int32, square, 0) == lax.broadcasted_iota(jnp.int32, square, 1)
    cinv_turned[...] = lax.dot_general(
        jnp.where(same, 1.0, 0.0), cinv_pad[...], contract_last, precision=highest, preferred_element_type=f32
    )

    weights = 1.0 / (1.0 + code_ref[...].astype(f32))
    load_inverse.wait()
    chunk = 32

    def split_rows(number, carry):
        at = pl.ds(pl.multiple_of(number * chunk, chunk), chunk)
        high, low = split(li[at, :] * weights)
        li_hi[at, :] = high
        li_lo[at, :] = low
        return carry

    lax.fori_loop(0, block // chunk, split_rows, 0)
    pl.semaphore_wait(barrier, len(partners))

    def tab_copy(d):
        return remote(table, tables.at[d], tab_s.at[d], tab_r.at[d], (sub_at(direction_steps[d]), c))

    for d in range(DIRS):

        @pl.when(inside(direction_steps[d]))
        def _():
            tab_copy(d).start()

    def read_tables():
        for d in range(DIRS):

            @pl.when(inside(direction_steps[d]))
            def _():
                tab_copy(d).wait_send()

            @pl.when(inside(-direction_steps[d]))
            def _():
                tab_copy(d).wait_recv()

        for d in range(DIRS):
            fidx[pl.ds(d, 1), :] = tables[d, pl.ds(d, 1), :]

        slot_number = lax.broadcasted_iota(jnp.int32, (LANES, LANES), 0).astype(f32) + 1.0
        lane_full = lax.broadcasted_iota(jnp.int32, (LANES, LANES), 1).astype(f32)
        for d in range(DIRS):
            wanted = jnp.broadcast_to(fidx[pl.ds(d, 1), :].astype(f32), (LANES, LANES)).T

            def invert(number, carry):
                hit = wanted == lane_full + lax.convert_element_type(number * LANES, f32)
                found = jnp.sum(jnp.where(hit, slot_number, 0.0), axis=0, keepdims=True)
                inverse[number, pl.ds(d, 1), :] = found.astype(jnp.int32) - 1
                return carry

            lax.fori_loop(0, tiles, invert, 0)

    def pack(read_tile, put):
        for d in range(DIRS):
            index = jnp.broadcast_to(fidx[pl.ds(d, 1), :], (rows, LANES))
            low, high = index & (LANES - 1), index >> 7
            total = jnp.zeros((rows, LANES), f32)
            for t in range(tiles):
                total = jnp.where(high == t, lane_gather(read_tile(t), low), total)
            put(d, total)

    def terms_over(sources, first, begin, stop, put):
        def at_tile(number, carry):
            at = pl.ds(pl.multiple_of(number * LANES, LANES), LANES)
            total = jnp.zeros((rows, LANES), f32)
            for k in range(terms):
                index = jnp.broadcast_to(idx_tiles[number, pl.ds(k, 1), :], (rows, LANES))
                low, high = index & (LANES - 1), index >> 7
                got = jnp.zeros((rows, LANES), f32)
                for t, tile in enumerate(sources):
                    got = jnp.where(high == first + t, lane_gather(tile, low), got)
                total = total + val_tiles[number, pl.ds(k, 1), :] * got
            put(at, total)
            return carry

        lax.fori_loop(begin, stop, at_tile, 0, unroll=2)

    own_parts = [max(0, min((b + 1) * block, owned) - b * block) for b in range(cols)]
    slot_homes = [divmod(owned + d * LANES, block) for d in range(DIRS)]

    def halo_copy(q, d):
        return remote(
            halo_out.at[q, d], halo_in.at[q, d], halo_s.at[q, d], halo_r.at[q, d], (sub_at(-direction_steps[d]), c)
        )

    def own_copy(q, part, step, slot):
        piece = own_x.at[q, slot, :, pl.ds(*cuts[part])]
        return remote(piece, piece, own_s.at[q, part, step], own_r.at[q, part, step], (s, col_at(step)))

    def mar_copy(q, d, step, slot):
        return remote(
            mar_out.at[q, d], mar_x.at[q, d, slot], mar_s.at[q, d, step], mar_r.at[q, d, step],
            (sub_at(-direction_steps[d]), col_at(step)),
        )

    def coarse_copy(q, by, slot):
        return remote(coarse_x.at[q, slot], coarse_x.at[q, slot], co_s.at[q, by], co_r.at[q, by], (sub_at(by), c))

    def sol_copy(q, b, step):
        width = own_parts[b]
        return remote(
            solved.at[q, col_at(step), :, pl.ds(0, width)], sol_in.at[q, b, :, pl.ds(0, width)],
            sol_s.at[q, step], sol_r.at[q, b], (s, col_at(step)),
        )

    def ret_copy(q, d, step):
        return remote(
            solved.at[q, col_at(step), :, pl.ds(slot_homes[d][1], LANES)], ret_in.at[q, d],
            ret_s.at[q, d, step], ret_r.at[q, d], (sub_at(direction_steps[d]), col_at(step)),
        )

    def each_return(act):
        for d in range(DIRS):

            @pl.when(jnp.logical_and(c == slot_homes[d][0], inside(direction_steps[d])))
            def _():
                for step in range(cols):
                    act(d, step)

    def halos(g, q):
        def put_halo(d, total):
            halo_out[q, d] = total

            @pl.when(inside(-direction_steps[d]))
            def _():
                halo_copy(q, d).start()

        pack(lambda t: lam[g, :, t * LANES : (t + 1) * LANES], put_halo)

    def begin(g, q):
        def put(at, total):
            own_x[q, c, :, at] = source_ref[pl.ds(g * rows, rows), at] - diag_ref[:, at] * lam[g, :, at] - total

        terms_over([lam[g, :, t * LANES : (t + 1) * LANES] for t in range(tiles)], 0, 0, early, put)

    def rest(g, q):
        for d in range(DIRS):

            @pl.when(inside(direction_steps[d]))
            def _():
                halo_copy(q, d).wait_recv()

        def put_more(at, total):
            own_x[q, c, :, at] = own_x[q, c, :, at] - total

        slots = [halo_in[q, d] for d in range(DIRS)]
        terms_over(slots, tiles, 0, early, put_more)
        for step in range(1, cols):
            own_copy(q, 0, step, c).start()

        def put(at, total):
            own_x[q, c, :, at] = source_ref[pl.ds(g * rows, rows), at] - diag_ref[:, at] * lam[g, :, at] - total

        terms_over([lam[g, :, t * LANES : (t + 1) * LANES] for t in range(tiles)] + slots, 0, early, tiles, put)

        def put_margin(d, total):
            mar_out[q, d] = total

            @pl.when(inside(-direction_steps[d]))
            def _():
                for step in range(cols):
                    mar_copy(q, d, step, c).start()

        pack(lambda t: own_x[q, c, :, t * LANES : (t + 1) * LANES], put_margin)
        for step in range(1, cols):
            own_copy(q, 1, step, c).start()
        message = jnp.zeros((rows, LANES), f32)
        for m in range(nmodes):
            part = jnp.zeros((rows, LANES), f32)
            for t in range(tiles):
                at = pl.ds(t * LANES, LANES)
                part = part + own_x[q, c, :, at] * modes_ref[pl.ds(m, 1), at]
            message = jnp.where(lane == m, jnp.sum(part, axis=1, keepdims=True), message)
        coarse_x[q, s] = message
        for by in range(1, subs):
            coarse_copy(q, by, s).start()

    def product(x, at):
        high, low = split(x)
        count = x.shape[0]
        both = lax.dot_general(
            jnp.concatenate([high, low], axis=0), li_hi[:, at], contract_last, preferred_element_type=f32
        )
        cross = lax.dot_general(high, li_lo[:, at], contract_last, preferred_element_type=f32)
        return both[:count] + (both[count:] + cross)

    def solve(q):
        for part in range(len(cuts)):
            for step in range(1, cols):
                own_copy(q, part, step, col_at(-step)).wait_recv()
        total = product(own_x[q].reshape(cols * rows, owned), pl.ds(0, owned))
        for d in range(DIRS):

            @pl.when(inside(direction_steps[d]))
            def _():
                for step in range(cols):
                    mar_copy(q, d, step, col_at(-step)).wait_recv()

        margins = jnp.concatenate([mar_x[q, d].reshape(cols * rows, LANES) for d in range(DIRS)], axis=1)
        total = total + product(margins, pl.ds(owned, DIRS * LANES))
        solved[q] = total.reshape(cols, rows, block)
        each_return(lambda d, step: ret_copy(q, d, step).start())
        for b in range(cols):
            if own_parts[b]:

                @pl.when(c == b)
                def _():
                    for step in range(1, cols):
                        sol_copy(q, b, step).start()
                    sol_in[q, b, :, pl.ds(0, own_parts[b])] = solved[q, c, :, pl.ds(0, own_parts[b])]

    def update(g, q):
        for by in range(1, subs):
            coarse_copy(q, by, sub_at(-by)).wait_recv()
        coarse = jnp.zeros((rows, LANES), f32)
        for other in range(subs):
            message = coarse_x[q, other]
            for m in range(nmodes):
                coarse = coarse + message[:, m : m + 1] * cinv_turned[pl.ds(other * nmodes + m, 1), :]
        levels = [jnp.broadcast_to(coarse[:, m : m + 1], (rows, LANES)) for m in range(nmodes)]
        for b in range(cols):
            if own_parts[b]:

                @pl.when(c != b)
                def _():
                    sol_copy(q, b, 0).wait_recv()

        for d in range(DIRS):

            @pl.when(inside(-direction_steps[d]))
            def _():
                ret_copy(q, d, 0).wait_recv()

        for t in range(tiles):
            at = pl.ds(t * LANES, LANES)
            b, offset = divmod(t * LANES, block)
            total = sol_in[q, b, :, pl.ds(offset, LANES)]
            for d in range(DIRS):
                index = jnp.broadcast_to(inverse[t, pl.ds(d, 1), :], (rows, LANES))
                total = total + jnp.where(index >= 0, lane_gather(ret_in[q, d], index & (LANES - 1)), 0.0)
            for m in range(nmodes):
                total = total + levels[m] * modes_ref[pl.ds(m, 1), at]
            lam[g, :, at] = lam[g, :, at] + damping * total

    last = GROUPS - 1

    def iteration(it, carry):
        q = it * GROUPS
        for g in range(GROUPS):
            update(g, q - GROUPS + g)
            halos(g, q + g)
            begin(g, q + g)
            solve(q + g - 1)
            rest(g, q + g)
        return carry

    for g in range(GROUPS):
        if g == 0:
            begin(g, g)
            read_tables()
            halos(g, g)
        else:
            halos(g, g)
            begin(g, g)
            solve(g - 1)
        rest(g, g)
    lax.fori_loop(1, ITERS, iteration, 0)
    final = (ITERS - 1) * GROUPS
    for g in range(last):
        update(g, final + g)
    solve(final + last)
    update(last, final + last)
    for g in range(GROUPS):
        out_ref[g * rows : (g + 1) * rows, :] = lam[g]

    def drain(q, carry):
        for d in range(DIRS):

            @pl.when(inside(-direction_steps[d]))
            def _():
                halo_copy(q, d).wait_send()
                for step in range(cols):
                    mar_copy(q, d, step, c).wait_send()

        for step in range(1, cols):
            for part in range(len(cuts)):
                own_copy(q, part, step, c).wait_send()
        for by in range(1, subs):
            coarse_copy(q, by, s).wait_send()
        each_return(lambda d, step: ret_copy(q, d, step).wait_send())
        for b in range(cols):
            if own_parts[b]:

                @pl.when(c == b)
                def _():
                    for step in range(1, cols):
                        sol_copy(q, b, step).wait_send()

        return carry

    lax.fori_loop(0, ITERS * GROUPS, drain, 0)


def local(
    subs, cols,
    adjoint_source,
    start_field,
    row_diagonal,
    row_values,
    row_columns,
    weight_code,
    slot_count,
    slot_rows,
    local_inverse,
    coarse_modes,
    coarse_inverse,
):
    ncol, owned = start_field.shape
    block, ext = local_inverse.shape
    rows = ncol // GROUPS
    rounds = ITERS * GROUPS
    vmem = pl.BlockSpec(memory_space=pltpu.VMEM)
    dma = pltpu.SemaphoreType.DMA
    return pl.pallas_call(
        functools.partial(kernel, subs, cols),
        out_shape=jax.ShapeDtypeStruct((ncol, owned), f32),
        in_specs=[vmem] * 6 + [pl.BlockSpec(memory_space=pltpu.SMEM)] + [vmem] * 3 + [pl.BlockSpec(memory_space=pl.ANY)],
        out_specs=vmem,
        scratch_shapes=[
            pltpu.VMEM((GROUPS, rows, owned), f32),
            pltpu.VMEM((owned // LANES, row_values.shape[0], LANES), jnp.int32),
            pltpu.VMEM((owned // LANES, row_values.shape[0], LANES), f32),
            pltpu.VMEM((block, ext), f32),
            pltpu.VMEM((block, ext), bf16),
            pltpu.VMEM((block, ext), bf16),
            pltpu.VMEM((SUBLANES, LANES), jnp.int32),
            pltpu.VMEM((DIRS, SUBLANES, LANES), jnp.int32),
            pltpu.VMEM((SUBLANES, LANES), jnp.int32),
            pltpu.VMEM((owned // LANES, SUBLANES, LANES), jnp.int32),
            pltpu.VMEM((LANES, coarse_inverse.shape[1]), f32),
            pltpu.VMEM((coarse_inverse.shape[1], LANES), f32),
            pltpu.VMEM((rounds, DIRS, rows, LANES), f32),
            pltpu.VMEM((rounds, DIRS, rows, LANES), f32),
            pltpu.VMEM((rounds, cols, rows, owned), f32),
            pltpu.VMEM((rounds, DIRS, rows, LANES), f32),
            pltpu.VMEM((rounds, DIRS, cols, rows, LANES), f32),
            pltpu.VMEM((rounds, subs, rows, LANES), f32),
            pltpu.VMEM((rounds, cols, rows, block), f32),
            pltpu.VMEM((rounds, cols, rows, block), f32),
            pltpu.VMEM((rounds, DIRS, rows, LANES), f32),
            dma,
            dma((DIRS,)),
            dma((DIRS,)),
            dma((rounds, DIRS)),
            dma((rounds, DIRS)),
            dma((rounds, 2, cols)),
            dma((rounds, 2, cols)),
            dma((rounds, DIRS, cols)),
            dma((rounds, DIRS, cols)),
            dma((rounds, subs)),
            dma((rounds, subs)),
            dma((rounds, cols)),
            dma((rounds, cols)),
            dma((rounds, DIRS, cols)),
            dma((rounds, DIRS)),
        ],
        compiler_params=pltpu.CompilerParams(collective_id=0, has_side_effects=True),
    )(
        adjoint_source,
        start_field,
        row_diagonal.reshape(1, owned),
        row_values,
        row_columns,
        weight_code.reshape(1, ext),
        slot_count,
        slot_rows,
        coarse_modes,
        coarse_inverse,
        local_inverse,
    )


def solution(mesh):
    return jax.shard_map(
        functools.partial(local, mesh.shape["sub"], mesh.shape["col"]),
        mesh=mesh,
        in_specs=(
            P("col", "sub"),
            P("col", "sub"),
            P("sub"),
            P(None, "sub"),
            P(None, "sub"),
            P("sub"),
            P("sub", None),
            P("sub", None, None),
            P(("sub", "col"), None),
            P(None, "sub"),
            P("sub", None),
        ),
        out_specs=P("col", "sub"),
        check_vma=False,
    )
```

profile of v0, /device:TPU:0, one launch (start us, length us, event | category | flops | bytes accessed | tf_op | source)
XLA Modules:
  0.0 88.4 jit_solution(10112401463411435113)
XLA Ops:
  0.0 1.3 %reshape.6.diag_ref = f32[1,1536]{1,0:T(1,128)} reshape(f32[1536]{0:T(1024)} %param.13) | data formatting | bytes 12288 | tf_op jit(solution)/shard_map/reshape | solution.py:470
  1.3 85.6 %shard_map.109 = f32[16,1536]{1,0:T(8,128)} custom-call(f32[16,1536]{1,0:T(8,128)} %source_ref.1, f32[16,1536]{1,0:T(8,128)} %start_ref.1, f32[1,1536]{1,0:T(1,128)} %reshape.6.diag_ref, f32[26,1536]{1,0:T(8,128)} %vals_ref.1, s32[26,1536]{1,0:T(8,128)} %idx_ref.1, s32[1,2048]{1,0:T(1,128)} %bitcast.1, s32[1,4]{1,0:T(1,128)} %count_ref.1, ...), custom_call_target="tpu_custom_call" | custom-call | tf_op jit(solution)/shard_map/pallas_call | solution.py:423
  86.9 1.5 %copy.13 = f32[16,1536]{1,0:T(8,128)} copy(f32[16,1536]{1,0:T(8,128)} %shard_map.109) | data formatting | bytes 196608
where the time goes:
time: 88.6 us; the launch traced here: 88.4 us
  Pallas kernels  85.6 us (97%)
  local copies, waits for them, and re-layouts  2.83 us (3%)
    pallas_call x1, Pallas kernels, local(): pl.pallas_call(functools.partial(kernel, subs, cols), out_shape=jax.Shape...  85.6 us

commit v1 on v0

--- a/solution.py
+++ b/solution.py
@@ -15,10 +15,11 @@
 damping = 0.7
 highest = lax.Precision.HIGHEST
 contract_last = (((1,), (1,)), ((), ()))
+contract_first = (((1,), (0,)), ((), ()))
 f32 = jnp.float32
 bf16 = jnp.bfloat16
 DIRS = len(direction_steps)
-GROUPS = 2
+GROUPS = 1
 
 
 def lane_gather(tile, low):
@@ -28,13 +29,98 @@
 def split(x):
     high = x.astype(bf16)
     return high, (x - high.astype(f32)).astype(bf16)
+
+
+def build_operator(idx_ref, vals_ref, op_hi, op_lo, turned, low_rows):
+    terms, owned = idx_ref.shape
+    heads = op_hi.shape[0] // LANES
+    tiles = owned // LANES
+    width = 1 << (terms - 1).bit_length()
+    per = LANES // width
+    halves = SUBLANES // per
+    blocks = LANES // SUBLANES
+    full = (LANES, LANES)
+    square_row = lax.broadcasted_iota(jnp.int32, full, 0)
+    square_lane = lax.broadcasted_iota(jnp.int32, full, 1)
+    eye = jnp.where(square_row == square_lane, 1.0, 0.0).astype(bf16)
+    keep = [square_row % SUBLANES == square_lane // width + per * h for h in range(halves)]
+    few = (blocks, LANES)
+    pick = lax.broadcasted_iota(jnp.int32, few, 1) // SUBLANES == lax.broadcasted_iota(jnp.int32, few, 0)
+    pick = jnp.where(pick, 1.0, 0.0).astype(bf16)
+
+    def turn(t, carry):
+        at = pl.ds(pl.multiple_of(t * LANES, LANES), LANES)
+        index, value = idx_ref[:, at], vals_ref[:, at]
+
+        def tiled(x, fill):
+            x = jnp.concatenate([x, jnp.full((width - terms, LANES), fill, f32)], axis=0)
+            return jnp.concatenate([x] * per, axis=0).astype(bf16)
+
+        def turn_one(x):
+            return lax.dot_general(eye, x, contract_last, preferred_element_type=f32)
+
+        top = value.astype(bf16).astype(f32)
+        turned[0, at, :] = turn_one(tiled((index >> 7).astype(f32), -1.0))
+        turned[1, at, :] = turn_one(tiled(top, 0.0))
+        turned[2, at, :] = turn_one(tiled(value - top, 0.0))
+        low = turn_one(tiled((index & (LANES - 1)).astype(f32), -1.0))
+        for h in range(halves):
+            low_rows[h, pl.ds(pl.multiple_of(t * blocks, blocks), blocks), :] = lax.dot_general(
+                pick, jnp.where(keep[h], low, 0.0).astype(bf16), contract_first, preferred_element_type=f32
+            )
+        return carry
+
+    lax.fori_loop(0, tiles, turn, 0, unroll=tiles)
+
+    lane_number = square_row.astype(f32).astype(bf16)
+    tall = (heads * SUBLANES, LANES)
+    head_number = (lax.broadcasted_iota(jnp.int32, tall, 0) // SUBLANES).astype(f32).astype(bf16)
+    small = (SUBLANES, LANES)
+    mine = [
+        lax.broadcasted_iota(jnp.int32, small, 0) == lax.broadcasted_iota(jnp.int32, small, 1) // width + per * h
+        for h in range(halves)
+    ]
+    one, zero = jnp.ones(full, bf16), jnp.zeros(full, bf16)
+    none = jnp.zeros(tall, bf16)
+
+    def repeat(x):
+        pair = jnp.concatenate([x, x], axis=0).astype(bf16)
+        return jnp.concatenate([pair] * (heads // 2), axis=0)
+
+    def one_block(row):
+        at = pl.ds(pl.multiple_of(row * SUBLANES, SUBLANES), SUBLANES)
+        head = turned[0, at, :]
+        value_hi, value_lo = repeat(turned[1, at, :]), repeat(turned[2, at, :])
+        left_hi, left_lo, right = [], [], []
+        for h in range(halves):
+            hit = repeat(jnp.where(mine[h], head, -1.0)) == head_number
+            left_hi.append(jnp.where(hit, value_hi, none))
+            left_lo.append(jnp.where(hit, value_lo, none))
+            low = jnp.broadcast_to(low_rows[h, pl.ds(row, 1), :], (2 * SUBLANES, LANES)).astype(bf16)
+            low = jnp.concatenate([low] * (LANES // (2 * SUBLANES)), axis=0)
+            right.append(jnp.where(low == lane_number, one, zero))
+        left = jnp.concatenate([jnp.concatenate(left_hi, axis=1), jnp.concatenate(left_lo, axis=1)], axis=0)
+        out = lax.dot_general(left, jnp.concatenate(right, axis=1), contract_last, preferred_element_type=f32)
+        return out[: heads * SUBLANES] + out[heads * SUBLANES :]
+
+    def one_tile(t, carry):
+        at = pl.ds(pl.multiple_of(t * LANES, LANES), LANES)
+        outs = [one_block(t * blocks + b) for b in range(blocks)]
+        for h in range(heads):
+            x = jnp.concatenate([out[h * SUBLANES : (h + 1) * SUBLANES] for out in outs], axis=0).T
+            high, low = split(x)
+            op_hi[h * LANES : (h + 1) * LANES, at] = high
+            op_lo[h * LANES : (h + 1) * LANES, at] = low
+        return carry
+
+    lax.fori_loop(0, tiles, one_tile, 0, unroll=2)
 
 
 def kernel(
     subs, cols,
     source_ref, start_ref, diag_ref, vals_ref, idx_ref, code_ref, count_ref, rows_ref, modes_ref, cinv_ref, li_hbm,
     out_ref,
-    lam, idx_tiles, val_tiles, li, li_hi, li_lo, table, tables, fidx, inverse, cinv_pad, cinv_turned,
+    lam, base, op_hi, op_lo, turned, low_rows, li, li_hi, li_lo, table, tables, fidx, inverse, cinv_pad, cinv_turned,
     halo_out, halo_in, own_x, mar_out, mar_x, coarse_x, solved, sol_in, ret_in,
     li_sem, tab_s, tab_r, halo_s, halo_r, own_s, own_r, mar_s, mar_r, co_s, co_r, sol_s, sol_r, ret_s, ret_r,
 ):
@@ -44,7 +130,6 @@
     rows = lam.shape[1]
     tiles = owned // LANES
     early = tiles // 2
-    terms = vals_ref.shape[0]
     block = li_hbm.shape[0]
     nmodes = modes_ref.shape[0]
     cuts = ((0, early * LANES), (early * LANES, owned - early * LANES))
@@ -87,9 +172,6 @@
         table[pl.ds(d, 1), :] = jnp.where(lane < count_ref[0, d], rows_ref[0, pl.ds(d, 1), :], -1)
     for g in range(GROUPS):
         lam[g] = start_ref[g * rows : (g + 1) * rows, :]
-    for t in range(tiles):
-        idx_tiles[t] = idx_ref[:, t * LANES : (t + 1) * LANES]
-        val_tiles[t] = vals_ref[:, t * LANES : (t + 1) * LANES]
     members = subs * nmodes
     cinv_pad[...] = jnp.zeros_like(cinv_pad)
     cinv_pad[pl.ds(0, nmodes), :] = cinv_ref[...]
@@ -99,18 +181,6 @@
         jnp.where(same, 1.0, 0.0), cinv_pad[...], contract_last, precision=highest, preferred_element_type=f32
     )
 
-    weights = 1.0 / (1.0 + code_ref[...].astype(f32))
-    load_inverse.wait()
-    chunk = 32
-
-    def split_rows(number, carry):
-        at = pl.ds(pl.multiple_of(number * chunk, chunk), chunk)
-        high, low = split(li[at, :] * weights)
-        li_hi[at, :] = high
-        li_lo[at, :] = low
-        return carry
-
-    lax.fori_loop(0, block // chunk, split_rows, 0)
     pl.semaphore_wait(barrier, len(partners))
 
     def tab_copy(d):
@@ -158,21 +228,13 @@
                 total = jnp.where(high == t, lane_gather(read_tile(t), low), total)
             put(d, total)
 
-    def terms_over(sources, first, begin, stop, put):
-        def at_tile(number, carry):
-            at = pl.ds(pl.multiple_of(number * LANES, LANES), LANES)
-            total = jnp.zeros((rows, LANES), f32)
-            for k in range(terms):
-                index = jnp.broadcast_to(idx_tiles[number, pl.ds(k, 1), :], (rows, LANES))
-                low, high = index & (LANES - 1), index >> 7
-                got = jnp.zeros((rows, LANES), f32)
-                for t, tile in enumerate(sources):
-                    got = jnp.where(high == first + t, lane_gather(tile, low), got)
-                total = total + val_tiles[number, pl.ds(k, 1), :] * got
-            put(at, total)
-            return carry
-
-        lax.fori_loop(begin, stop, at_tile, 0, unroll=2)
+    def operate(x, low, high, at):
+        count = x.shape[0]
+        top, bottom = split(x)
+        stretch = pl.ds(low, high - low)
+        both = jnp.dot(jnp.concatenate([top, bottom], axis=0), op_hi[stretch, at], preferred_element_type=f32)
+        cross = jnp.dot(top, op_lo[stretch, at], preferred_element_type=f32)
+        return both[:count] + (both[count:] + cross)
 
     own_parts = [max(0, min((b + 1) * block, owned) - b * block) for b in range(cols)]
     slot_homes = [divmod(owned + d * LANES, block) for d in range(DIRS)]
@@ -227,10 +289,10 @@
         pack(lambda t: lam[g, :, t * LANES : (t + 1) * LANES], put_halo)
 
     def begin(g, q):
-        def put(at, total):
-            own_x[q, c, :, at] = source_ref[pl.ds(g * rows, rows), at] - diag_ref[:, at] * lam[g, :, at] - total
-
-        terms_over([lam[g, :, t * LANES : (t + 1) * LANES] for t in range(tiles)], 0, 0, early, put)
+        for low, count in cuts:
+            at = pl.ds(low, count)
+            held = lam[g, :, at]
+            base[:, at] = source_ref[g * rows : (g + 1) * rows, at] - diag_ref[:, at] * held - operate(lam[g], 0, owned, at)
 
     def rest(g, q):
         for d in range(DIRS):
@@ -239,18 +301,12 @@
             def _():
                 halo_copy(q, d).wait_recv()
 
-        def put_more(at, total):
-            own_x[q, c, :, at] = own_x[q, c, :, at] - total
-
-        slots = [halo_in[q, d] for d in range(DIRS)]
-        terms_over(slots, tiles, 0, early, put_more)
-        for step in range(1, cols):
-            own_copy(q, 0, step, c).start()
-
-        def put(at, total):
-            own_x[q, c, :, at] = source_ref[pl.ds(g * rows, rows), at] - diag_ref[:, at] * lam[g, :, at] - total
-
-        terms_over([lam[g, :, t * LANES : (t + 1) * LANES] for t in range(tiles)] + slots, 0, early, tiles, put)
+        slots = jnp.concatenate([halo_in[q, d] for d in range(DIRS)], axis=1)
+        for part, (low, count) in enumerate(cuts):
+            at = pl.ds(low, count)
+            own_x[q, c, :, at] = base[:, at] - operate(slots, owned, owned + DIRS * LANES, at)
+            for step in range(1, cols):
+                own_copy(q, part, step, c).start()
 
         def put_margin(d, total):
             mar_out[q, d] = total
@@ -261,8 +317,6 @@
                     mar_copy(q, d, step, c).start()
 
         pack(lambda t: own_x[q, c, :, t * LANES : (t + 1) * LANES], put_margin)
-        for step in range(1, cols):
-            own_copy(q, 1, step, c).start()
         message = jnp.zeros((rows, LANES), f32)
         for m in range(nmodes):
             part = jnp.zeros((rows, LANES), f32)
@@ -341,34 +395,34 @@
                 total = total + levels[m] * modes_ref[pl.ds(m, 1), at]
             lam[g, :, at] = lam[g, :, at] + damping * total
 
-    last = GROUPS - 1
-
     def iteration(it, carry):
-        q = it * GROUPS
-        for g in range(GROUPS):
-            update(g, q - GROUPS + g)
-            halos(g, q + g)
-            begin(g, q + g)
-            solve(q + g - 1)
-            rest(g, q + g)
+        update(0, it - 1)
+        halos(0, it)
+        begin(0, it)
+        rest(0, it)
+        solve(it)
         return carry
 
-    for g in range(GROUPS):
-        if g == 0:
-            begin(g, g)
-            read_tables()
-            halos(g, g)
-        else:
-            halos(g, g)
-            begin(g, g)
-            solve(g - 1)
-        rest(g, g)
+    read_tables()
+    halos(0, 0)
+    build_operator(idx_ref, vals_ref, op_hi, op_lo, turned, low_rows)
+    weights = 1.0 / (1.0 + code_ref[...].astype(f32))
+    load_inverse.wait()
+    chunk = 32
+
+    def split_rows(number, carry):
+        at = pl.ds(pl.multiple_of(number * chunk, chunk), chunk)
+        high, low = split(li[at, :] * weights)
+        li_hi[at, :] = high
+        li_lo[at, :] = low
+        return carry
+
+    lax.fori_loop(0, block // chunk, split_rows, 0)
+    begin(0, 0)
+    rest(0, 0)
+    solve(0)
     lax.fori_loop(1, ITERS, iteration, 0)
-    final = (ITERS - 1) * GROUPS
-    for g in range(last):
-        update(g, final + g)
-    solve(final + last)
-    update(last, final + last)
+    update(0, ITERS - 1)
     for g in range(GROUPS):
         out_ref[g * rows : (g + 1) * rows, :] = lam[g]
 
@@ -427,8 +481,11 @@
         out_specs=vmem,
         scratch_shapes=[
             pltpu.VMEM((GROUPS, rows, owned), f32),
-            pltpu.VMEM((owned // LANES, row_values.shape[0], LANES), jnp.int32),
-            pltpu.VMEM((owned // LANES, row_values.shape[0], LANES), f32),
+            pltpu.VMEM((rows, owned), f32),
+            pltpu.VMEM((ext, owned), bf16),
+            pltpu.VMEM((ext, owned), bf16),
+            pltpu.VMEM((3, owned, LANES), f32),
+            pltpu.VMEM((SUBLANES // (LANES // (1 << (row_values.shape[0] - 1).bit_length())), owned // SUBLANES, LANES), f32),
             pltpu.VMEM((block, ext), f32),
             pltpu.VMEM((block, ext), bf16),
             pltpu.VMEM((block, ext), bf16),

time: 88.6 us -> 75.6 us (0.85)
  Pallas kernels: 85.6 us -> 72.5 us
    pallas_call x1, Pallas kernels: 85.6 us -> 72.5 us  [local(): pl.pallas_call(functools.partial(kernel, subs, cols), out_shape=jax.Shape...]
where the time goes in v1:
time: 75.6 us; the launch traced here: 75.4 us
  Pallas kernels  72.5 us (96%)
  local copies, waits for them, and re-layouts  2.83 us (4%)
    pallas_call x1, Pallas kernels, local(): pl.pallas_call(functools.partial(kernel, subs, cols), out_shape=jax.Shape...  72.5 us
    unnamed x1, local copies, waits for them, and re-layouts  1.54 us

profile of v1, /device:TPU:0, one launch (start us, length us, event | category | flops | bytes accessed | tf_op | source)
XLA Modules:
  0.0 75.4 jit_solution(12343088457003114184)
XLA Ops:
  0.0 1.3 %reshape.6.diag_ref = f32[1,1536]{1,0:T(1,128)} reshape(f32[1536]{0:T(1024)} %param.13) | data formatting | bytes 12288 | tf_op jit(solution)/shard_map/reshape | solution.py:527
  1.3 72.5 %shard_map.109 = f32[16,1536]{1,0:T(8,128)} custom-call(f32[16,1536]{1,0:T(8,128)} %source_ref.1, f32[16,1536]{1,0:T(8,128)} %start_ref.1, f32[1,1536]{1,0:T(1,128)} %reshape.6.diag_ref, f32[26,1536]{1,0:T(8,128)} %vals_ref.1, s32[26,1536]{1,0:T(8,128)} %idx_ref.1, s32[1,2048]{1,0:T(1,128)} %bitcast.1, s32[1,4]{1,0:T(1,128)} %count_ref.1, ...), custom_call_target="tpu_custom_call" | custom-call | tf_op jit(solution)/shard_map/pallas_call | solution.py:477
  73.8 1.5 %copy.13 = f32[16,1536]{1,0:T(8,128)} copy(f32[16,1536]{1,0:T(8,128)} %shard_map.109) | data formatting | bytes 196608

commit v2 on v1

--- a/solution.py
+++ b/solution.py
@@ -31,7 +31,7 @@
     return high, (x - high.astype(f32)).astype(bf16)
 
 
-def build_operator(idx_ref, vals_ref, op_hi, op_lo, turned, low_rows):
+def build_operator(idx_ref, vals_ref, op_hi, op_lo, turned, low_rows, halfway, later):
     terms, owned = idx_ref.shape
     heads = op_hi.shape[0] // LANES
     tiles = owned // LANES
@@ -72,6 +72,7 @@
 
     lax.fori_loop(0, tiles, turn, 0, unroll=tiles)
 
+    halfway()
     lane_number = square_row.astype(f32).astype(bf16)
     tall = (heads * SUBLANES, LANES)
     head_number = (lax.broadcasted_iota(jnp.int32, tall, 0) // SUBLANES).astype(f32).astype(bf16)
@@ -113,14 +114,17 @@
             op_lo[h * LANES : (h + 1) * LANES, at] = low
         return carry
 
-    lax.fori_loop(0, tiles, one_tile, 0, unroll=2)
+    early = tiles // 4 * 2
+    lax.fori_loop(0, early, one_tile, 0, unroll=2)
+    later()
+    lax.fori_loop(early, tiles, one_tile, 0, unroll=2)
 
 
 def kernel(
     subs, cols,
     source_ref, start_ref, diag_ref, vals_ref, idx_ref, code_ref, count_ref, rows_ref, modes_ref, cinv_ref, li_hbm,
     out_ref,
-    lam, base, op_hi, op_lo, turned, low_rows, li, li_hi, li_lo, table, tables, fidx, inverse, cinv_pad, cinv_turned,
+    lam, base, op_hi, op_lo, turned, low_rows, li, li_hi, li_lo, weights_ref, table, tables, fidx, inverse, cinv_pad, cinv_turned,
     halo_out, halo_in, own_x, mar_out, mar_x, coarse_x, solved, sol_in, ret_in,
     li_sem, tab_s, tab_r, halo_s, halo_r, own_s, own_r, mar_s, mar_r, co_s, co_r, sol_s, sol_r, ret_s, ret_r,
 ):
@@ -181,16 +185,16 @@
         jnp.where(same, 1.0, 0.0), cinv_pad[...], contract_last, precision=highest, preferred_element_type=f32
     )
 
-    pl.semaphore_wait(barrier, len(partners))
-
     def tab_copy(d):
         return remote(table, tables.at[d], tab_s.at[d], tab_r.at[d], (sub_at(direction_steps[d]), c))
 
-    for d in range(DIRS):
-
-        @pl.when(inside(direction_steps[d]))
-        def _():
-            tab_copy(d).start()
+    def send_tables():
+        pl.semaphore_wait(barrier, len(partners))
+        for d in range(DIRS):
+
+            @pl.when(inside(direction_steps[d]))
+            def _():
+                tab_copy(d).start()
 
     def read_tables():
         for d in range(DIRS):
@@ -244,9 +248,24 @@
             halo_out.at[q, d], halo_in.at[q, d], halo_s.at[q, d], halo_r.at[q, d], (sub_at(-direction_steps[d]), c)
         )
 
+    sibling = c + 1 - 2 * lax.rem(c, 2)
+
     def own_copy(q, part, step, slot):
         piece = own_x.at[q, slot, :, pl.ds(*cuts[part])]
-        return remote(piece, piece, own_s.at[q, part, step], own_r.at[q, part, step], (s, col_at(step)))
+        where = sibling if step % 2 else col_at(step)
+        return remote(piece, piece, own_s.at[q, part, step], own_r.at[q, part, step], (s, where))
+
+    def passed(step):
+        return c if step == 1 else col_at(1 - step)
+
+    def came(step):
+        return lax.rem(sibling + (1 - step + cols), cols) if step % 2 else col_at(-step)
+
+    def forward(q):
+        for part in range(len(cuts)):
+            for step in range(2, cols, 2):
+                own_copy(q, part, step, came(step)).wait_recv()
+                own_copy(q, part, step + 1, passed(step + 1)).start()
 
     def mar_copy(q, d, step, slot):
         return remote(
@@ -305,7 +324,7 @@
         for part, (low, count) in enumerate(cuts):
             at = pl.ds(low, count)
             own_x[q, c, :, at] = base[:, at] - operate(slots, owned, owned + DIRS * LANES, at)
-            for step in range(1, cols):
+            for step in [*range(2, cols, 2), 1]:
                 own_copy(q, part, step, c).start()
 
         def put_margin(d, total):
@@ -331,17 +350,17 @@
     def product(x, at):
         high, low = split(x)
         count = x.shape[0]
-        both = lax.dot_general(
-            jnp.concatenate([high, low], axis=0), li_hi[:, at], contract_last, preferred_element_type=f32
-        )
-        cross = lax.dot_general(high, li_lo[:, at], contract_last, preferred_element_type=f32)
+        both = jnp.dot(jnp.concatenate([high, low], axis=0), li_hi[at, :], preferred_element_type=f32)
+        cross = jnp.dot(high, li_lo[at, :], preferred_element_type=f32)
         return both[:count] + (both[count:] + cross)
 
     def solve(q):
-        for part in range(len(cuts)):
-            for step in range(1, cols):
-                own_copy(q, part, step, col_at(-step)).wait_recv()
-        total = product(own_x[q].reshape(cols * rows, owned), pl.ds(0, owned))
+        total = jnp.zeros((cols * rows, block), f32)
+        for part, (low, count) in enumerate(cuts):
+            for step in range(1, cols, 2):
+                own_copy(q, part, step, came(step)).wait_recv()
+            at = pl.ds(low, count)
+            total = total + product(own_x[q, :, :, at].reshape(cols * rows, count), at)
         for d in range(DIRS):
 
             @pl.when(inside(direction_steps[d]))
@@ -400,26 +419,32 @@
         halos(0, it)
         begin(0, it)
         rest(0, it)
+        forward(it)
         solve(it)
         return carry
 
-    read_tables()
-    halos(0, 0)
-    build_operator(idx_ref, vals_ref, op_hi, op_lo, turned, low_rows)
-    weights = 1.0 / (1.0 + code_ref[...].astype(f32))
+    def start_halos():
+        read_tables()
+        for g in range(GROUPS):
+            halos(g, g)
+
+    build_operator(idx_ref, vals_ref, op_hi, op_lo, turned, low_rows, send_tables, start_halos)
+    weights_ref[...] = 1.0 / (1.0 + code_ref[...].astype(f32))
     load_inverse.wait()
-    chunk = 32
-
-    def split_rows(number, carry):
-        at = pl.ds(pl.multiple_of(number * chunk, chunk), chunk)
-        high, low = split(li[at, :] * weights)
-        li_hi[at, :] = high
-        li_lo[at, :] = low
+
+    def split_tile(number, carry):
+        at = pl.ds(pl.multiple_of(number * LANES, LANES), LANES)
+        scale = weights_ref[:, at]
+        for low in range(0, block, LANES):
+            high, rest_of = split((li[low : low + LANES, at] * scale).T)
+            li_hi[at, low : low + LANES] = high
+            li_lo[at, low : low + LANES] = rest_of
         return carry
 
-    lax.fori_loop(0, block // chunk, split_rows, 0)
+    lax.fori_loop(0, li_hbm.shape[1] // LANES, split_tile, 0, unroll=2)
     begin(0, 0)
     rest(0, 0)
+    forward(0)
     solve(0)
     lax.fori_loop(1, ITERS, iteration, 0)
     update(0, ITERS - 1)
@@ -437,7 +462,7 @@
 
         for step in range(1, cols):
             for part in range(len(cuts)):
-                own_copy(q, part, step, c).wait_send()
+                own_copy(q, part, step, passed(step) if step % 2 else c).wait_send()
         for by in range(1, subs):
             coarse_copy(q, by, s).wait_send()
         each_return(lambda d, step: ret_copy(q, d, step).wait_send())
@@ -487,8 +512,9 @@
             pltpu.VMEM((3, owned, LANES), f32),
             pltpu.VMEM((SUBLANES // (LANES // (1 << (row_values.shape[0] - 1).bit_length())), owned // SUBLANES, LANES), f32),
             pltpu.VMEM((block, ext), f32),
-            pltpu.VMEM((block, ext), bf16),
-            pltpu.VMEM((block, ext), bf16),
+            pltpu.VMEM((ext, block), bf16),
+            pltpu.VMEM((ext, block), bf16),
+            pltpu.VMEM((1, ext), f32),
             pltpu.VMEM((SUBLANES, LANES), jnp.int32),
             pltpu.VMEM((DIRS, SUBLANES, LANES), jnp.int32),
             pltpu.VMEM((SUBLANES, LANES), jnp.int32),

time: 75.6 us -> 65.9 us (0.87)
  Pallas kernels: 72.5 us -> 62.8 us
    pallas_call x1, Pallas kernels: 72.5 us -> 62.8 us  [local(): pl.pallas_call(functools.partial(kernel, subs, cols), out_shape=jax.Shape...]
where the time goes in v2:
time: 65.9 us; the launch traced here: 65.7 us
  Pallas kernels  62.8 us (95%)
  local copies, waits for them, and re-layouts  2.83 us (4%)
    pallas_call x1, Pallas kernels, local(): pl.pallas_call(functools.partial(kernel, subs, cols), out_shape=jax.Shape...  62.8 us
    unnamed x1, local copies, waits for them, and re-layouts  1.54 us

profile of v2, /device:TPU:0, one launch (start us, length us, event | category | flops | bytes accessed | tf_op | source)
XLA Modules:
  0.0 65.7 jit_solution(15098622156302657632)
XLA Ops:
  0.0 1.3 %reshape.6.diag_ref = f32[1,1536]{1,0:T(1,128)} reshape(f32[1536]{0:T(1024)} %param.13) | data formatting | bytes 12288 | tf_op jit(solution)/shard_map/reshape | solution.py:553
  1.3 62.8 %shard_map.109 = f32[16,1536]{1,0:T(8,128)} custom-call(f32[16,1536]{1,0:T(8,128)} %source_ref.1, f32[16,1536]{1,0:T(8,128)} %start_ref.1, f32[1,1536]{1,0:T(1,128)} %reshape.6.diag_ref, f32[26,1536]{1,0:T(8,128)} %vals_ref.1, s32[26,1536]{1,0:T(8,128)} %idx_ref.1, s32[1,2048]{1,0:T(1,128)} %bitcast.1, s32[1,4]{1,0:T(1,128)} %count_ref.1, ...), custom_call_target="tpu_custom_call" | custom-call | tf_op jit(solution)/shard_map/pallas_call | solution.py:502
  64.1 1.5 %copy.13 = f32[16,1536]{1,0:T(8,128)} copy(f32[16,1536]{1,0:T(8,128)} %shard_map.109) | data formatting | bytes 196608

commit v3 on v2

--- a/solution.py
+++ b/solution.py
@@ -31,7 +31,7 @@
     return high, (x - high.astype(f32)).astype(bf16)
 
 
-def build_operator(idx_ref, vals_ref, op_hi, op_lo, turned, low_rows, halfway, later):
+def build_operator(idx_ref, vals_ref, op_hi, op_lo, turned, low_rows, halfway, later, beside):
     terms, owned = idx_ref.shape
     heads = op_hi.shape[0] // LANES
     tiles = owned // LANES
@@ -117,14 +117,19 @@
     early = tiles // 4 * 2
     lax.fori_loop(0, early, one_tile, 0, unroll=2)
     later()
-    lax.fori_loop(early, tiles, one_tile, 0, unroll=2)
+
+    def one_tile_beside(t, carry):
+        beside(t - early, tiles - early)
+        return one_tile(t, carry)
+
+    lax.fori_loop(early, tiles, one_tile_beside, 0, unroll=2)
 
 
 def kernel(
     subs, cols,
     source_ref, start_ref, diag_ref, vals_ref, idx_ref, code_ref, count_ref, rows_ref, modes_ref, cinv_ref, li_hbm,
     out_ref,
-    lam, base, op_hi, op_lo, turned, low_rows, li, li_hi, li_lo, weights_ref, table, tables, fidx, inverse, cinv_pad, cinv_turned,
+    lam, diag, base, op_hi, op_lo, turned, low_rows, li, li_hi, li_lo, weights_ref, table, tables, fidx, inverse, cinv_pad, cinv_turned,
     halo_out, halo_in, own_x, mar_out, mar_x, coarse_x, solved, sol_in, ret_in,
     li_sem, tab_s, tab_r, halo_s, halo_r, own_s, own_r, mar_s, mar_r, co_s, co_r, sol_s, sol_r, ret_s, ret_r,
 ):
@@ -133,10 +138,11 @@
     owned = start_ref.shape[1]
     rows = lam.shape[1]
     tiles = owned // LANES
-    early = tiles // 2
     block = li_hbm.shape[0]
     nmodes = modes_ref.shape[0]
-    cuts = ((0, early * LANES), (early * LANES, owned - early * LANES))
+    pieces = 3
+    edges = [tiles * n // pieces * LANES for n in range(pieces + 1)]
+    cuts = tuple((low, high - low) for low, high in zip(edges, edges[1:]))
 
     def sub_at(by):
         return lax.rem(s + (by + subs), subs)
@@ -174,6 +180,8 @@
     lane = lax.broadcasted_iota(jnp.int32, (1, LANES), 1)
     for d in range(DIRS):
         table[pl.ds(d, 1), :] = jnp.where(lane < count_ref[0, d], rows_ref[0, pl.ds(d, 1), :], -1)
+    for t in range(tiles):
+        diag[:, t * LANES : (t + 1) * LANES] = diag_ref[pl.ds(t * LANES, LANES)].reshape(1, LANES)
     for g in range(GROUPS):
         lam[g] = start_ref[g * rows : (g + 1) * rows, :]
     members = subs * nmodes
@@ -221,7 +229,7 @@
                 inverse[number, pl.ds(d, 1), :] = found.astype(jnp.int32) - 1
                 return carry
 
-            lax.fori_loop(0, tiles, invert, 0)
+            lax.fori_loop(0, tiles, invert, 0, unroll=4)
 
     def pack(read_tile, put):
         for d in range(DIRS):
@@ -311,7 +319,7 @@
         for low, count in cuts:
             at = pl.ds(low, count)
             held = lam[g, :, at]
-            base[:, at] = source_ref[g * rows : (g + 1) * rows, at] - diag_ref[:, at] * held - operate(lam[g], 0, owned, at)
+            base[:, at] = source_ref[g * rows : (g + 1) * rows, at] - diag[:, at] * held - operate(lam[g], 0, owned, at)
 
     def rest(g, q):
         for d in range(DIRS):
@@ -427,21 +435,26 @@
         read_tables()
         for g in range(GROUPS):
             halos(g, g)
-
-    build_operator(idx_ref, vals_ref, op_hi, op_lo, turned, low_rows, send_tables, start_halos)
-    weights_ref[...] = 1.0 / (1.0 + code_ref[...].astype(f32))
-    load_inverse.wait()
-
-    def split_tile(number, carry):
+        load_inverse.wait()
+
+    def split_tile(number):
         at = pl.ds(pl.multiple_of(number * LANES, LANES), LANES)
         scale = weights_ref[:, at]
         for low in range(0, block, LANES):
             high, rest_of = split((li[low : low + LANES, at] * scale).T)
             li_hi[at, low : low + LANES] = high
             li_lo[at, low : low + LANES] = rest_of
-        return carry
-
-    lax.fori_loop(0, li_hbm.shape[1] // LANES, split_tile, 0, unroll=2)
+
+    def split_beside(number, count):
+        pieces = li_hbm.shape[1] // LANES
+        each = -(-pieces // count)
+        for n in range(each):
+            split_tile(lax.rem(number * each + n, pieces))
+
+    weights_ref[...] = 1.0 / (1.0 + code_ref[...].astype(f32))
+    build_operator(
+        idx_ref, vals_ref, op_hi, op_lo, turned, low_rows, send_tables, start_halos, split_beside
+    )
     begin(0, 0)
     rest(0, 0)
     forward(0)
@@ -506,6 +519,7 @@
         out_specs=vmem,
         scratch_shapes=[
             pltpu.VMEM((GROUPS, rows, owned), f32),
+            pltpu.VMEM((1, owned), f32),
             pltpu.VMEM((rows, owned), f32),
             pltpu.VMEM((ext, owned), bf16),
             pltpu.VMEM((ext, owned), bf16),
@@ -535,8 +549,8 @@
             dma((DIRS,)),
             dma((rounds, DIRS)),
             dma((rounds, DIRS)),
-            dma((rounds, 2, cols)),
-            dma((rounds, 2, cols)),
+            dma((rounds, 3, cols)),
+            dma((rounds, 3, cols)),
             dma((rounds, DIRS, cols)),
             dma((rounds, DIRS, cols)),
             dma((rounds, subs)),
@@ -550,7 +564,7 @@
     )(
         adjoint_source,
         start_field,
-        row_diagonal.reshape(1, owned),
+        row_diagonal,
         row_values,
         row_columns,
         weight_code.reshape(1, ext),

time: 65.9 us -> 61.6 us (0.935)
  Pallas kernels: 62.8 us -> 59.9 us
  local copies, waits for them, and re-layouts: 2.83 us -> 1.54 us
    pallas_call x1, Pallas kernels: 62.8 us -> 59.9 us  [local(): pl.pallas_call(functools.partial(kernel, subs, cols), out_shape=jax.Shape...]
    reshape x1 -> x0, local copies, waits for them, and re-layouts: 1.29 us -> none  [local(): row_diagonal.reshape(1, owned)]
where the time goes in v3:
time: 61.6 us; the launch traced here: 61.4 us
  Pallas kernels  59.9 us (97%)
  local copies, waits for them, and re-layouts  1.54 us (2%)
    pallas_call x1, Pallas kernels, local(): pl.pallas_call(functools.partial(kernel, subs, cols), out_shape=jax.Shape...  59.9 us
    unnamed x1, local copies, waits for them, and re-layouts  1.54 us

profile of v3, /device:TPU:0, one launch (start us, length us, event | category | flops | bytes accessed | tf_op | source)
XLA Modules:
  0.0 61.4 jit_solution(8719485161709553837)
XLA Ops:
  0.0 59.9 %shard_map.109 = f32[16,1536]{1,0:T(8,128)} custom-call(f32[16,1536]{1,0:T(8,128)} %source_ref.1, f32[16,1536]{1,0:T(8,128)} %start_ref.1, f32[1536]{0:T(1024)} %diag_ref.1, f32[26,1536]{1,0:T(8,128)} %vals_ref.1, s32[26,1536]{1,0:T(8,128)} %idx_ref.1, s32[1,2048]{1,0:T(1,128)} %bitcast.1, s32[1,4]{1,0:T(1,128)} %count_ref.1, s32[1,4,128]{2,1,0:T(4,128)} %rows_ref.1, ...), custom_call_target="tpu_custom_call" | custom-call | tf_op jit(solution)/shard_map/pallas_call | solution.py:515
  59.9 1.5 %copy.13 = f32[16,1536]{1,0:T(8,128)} copy(f32[16,1536]{1,0:T(8,128)} %shard_map.109) | data formatting | bytes 196608

commit v4 on v3

--- a/solution.py
+++ b/solution.py
@@ -115,14 +115,14 @@
         return carry
 
     early = tiles // 4 * 2
-    lax.fori_loop(0, early, one_tile, 0, unroll=2)
+    lax.fori_loop(0, early, one_tile, 0, unroll=6)
     later()
 
     def one_tile_beside(t, carry):
         beside(t - early, tiles - early)
         return one_tile(t, carry)
 
-    lax.fori_loop(early, tiles, one_tile_beside, 0, unroll=2)
+    lax.fori_loop(early, tiles, one_tile_beside, 0, unroll=6)
 
 
 def kernel(

time: 61.6 us -> 59.3 us (0.963)
  Pallas kernels: 59.9 us -> 57.6 us
    pallas_call x1, Pallas kernels: 59.9 us -> 57.6 us  [local(): pl.pallas_call(functools.partial(kernel, subs, cols), out_shape=jax.Shape...]
where the time goes in v4:
time: 59.3 us; the launch traced here: 59.2 us
  Pallas kernels  57.6 us (97%)
  local copies, waits for them, and re-layouts  1.54 us (3%)
    pallas_call x1, Pallas kernels, local(): pl.pallas_call(functools.partial(kernel, subs, cols), out_shape=jax.Shape...  57.6 us
    unnamed x1, local copies, waits for them, and re-layouts  1.54 us

profile of v4, /device:TPU:0, one launch (start us, length us, event | category | flops | bytes accessed | tf_op | source)
XLA Modules:
  0.0 59.2 jit_solution(14126673825869206776)
XLA Ops:
  0.0 57.6 %shard_map.109 = f32[16,1536]{1,0:T(8,128)} custom-call(f32[16,1536]{1,0:T(8,128)} %source_ref.1, f32[16,1536]{1,0:T(8,128)} %start_ref.1, f32[1536]{0:T(1024)} %diag_ref.1, f32[26,1536]{1,0:T(8,128)} %vals_ref.1, s32[26,1536]{1,0:T(8,128)} %idx_ref.1, s32[1,2048]{1,0:T(1,128)} %bitcast.1, s32[1,4]{1,0:T(1,128)} %count_ref.1, s32[1,4,128]{2,1,0:T(4,128)} %rows_ref.1, ...), custom_call_target="tpu_custom_call" | custom-call | tf_op jit(solution)/shard_map/pallas_call | solution.py:515
  57.6 1.5 %copy.13 = f32[16,1536]{1,0:T(8,128)} copy(f32[16,1536]{1,0:T(8,128)} %shard_map.109) | data formatting | bytes 196608
